TPU v7x, 32 devices: a whole 2x2x4 slice. The times are simulated.
32 devices in a mesh: dp: 16 (over z, y, x), rep: 2 (over core).
Axes of the slice: x: 2, y: 2, z: 4, core: 2. Of those that a mesh axis runs over, the one named last changes fastest.
Arguments:
- long_clips: bfloat16 [2, 32, 1024, 768], P(None, ('dp', 'rep')), may hold values from -6 to 6
- short_clips: bfloat16 [2, 128, 64, 768], P(None, ('dp', 'rep')), may hold values from -6 to 6
- long_index: int32 [2, 32, 1024], P(None, ('dp', 'rep')), may hold values from 0 to 6271, as said below
- short_index: int32 [2, 128, 64], P(None, ('dp', 'rep')), may hold values from 0 to 6271, as said below
- long_length: int32 [2, 32], P(None, ('dp', 'rep')), may hold values from 128 to 1024, as said below
- short_length: int32 [2, 128], replicated, may hold values from 0 to 64, as said below
- destination: int32 [2, 128], replicated, may hold values from 0 to 15, as said below
- long_target: bfloat16 [2, 32, 1024, 1024], P(None, ('dp', 'rep')), may hold values from -6 to 6
- short_target: bfloat16 [2, 128, 64, 1024], P(None, ('dp', 'rep')), may hold values from -6 to 6
- position: bfloat16 [6272, 768], replicated, may hold values from -3 to 3
- mixer_gain: float32 [768], replicated, may hold values from 0.5 to 1.5
- mixer_shift: float32 [768], replicated, may hold values from -1 to 1
- heads_weight: bfloat16 [768, 2304], replicated, may hold values from -0.21875 to 0.21875
- query_bias: float32 [768], replicated, may hold values from -1 to 1
- value_bias: float32 [768], replicated, may hold values from -1 to 1
- out_weight: bfloat16 [768, 768], replicated, may hold values from -1.25 to 1.25
- out_bias: float32 [768], replicated, may hold values from -1 to 1
- dense_gain: float32 [768], replicated, may hold values from 0.5 to 1.5
- dense_shift: float32 [768], replicated, may hold values from -1 to 1
- up_weight: bfloat16 [768, 3072], replicated, may hold values from -0.21875 to 0.21875
- up_bias: float32 [3072], replicated, may hold values from -1 to 1
- down_weight: bfloat16 [3072, 768], replicated, may hold values from -0.109375 to 0.109375
- down_bias: float32 [768], replicated, may hold values from -1 to 1
- align_weight: bfloat16 [768, 1024], replicated, may hold values from -0.21875 to 0.21875
- align_bias: float32 [1024], replicated, may hold values from -1 to 1
Outputs:
- long_output: bfloat16 [2, 32, 1024, 768], P(None, ('dp', 'rep'))
- short_output: bfloat16 [2, 64, 64, 768], P(None, ('dp', 'rep'))
- long_grad: bfloat16 [2, 32, 1024, 768], P(None, ('dp', 'rep'))
- short_grad: bfloat16 [2, 128, 64, 768], P(None, ('dp', 'rep'))
- position_grad: float32 [6272, 768], P('dp')
- mixer_gain_grad: float32 [768], P('dp')
- mixer_shift_grad: float32 [768], P('dp')
- heads_weight_grad: float32 [768, 2304], P('dp')
- query_bias_grad: float32 [768], P('dp')
- value_bias_grad: float32 [768], P('dp')
- out_weight_grad: float32 [768, 768], P('dp')
- out_bias_grad: float32 [768], P('dp')
- dense_gain_grad: float32 [768], P('dp')
- dense_shift_grad: float32 [768], P('dp')
- up_weight_grad: float32 [768, 3072], P('dp')
- up_bias_grad: float32 [3072], P('dp')
- down_weight_grad: float32 [3072, 768], P('dp')
- down_bias_grad: float32 [768], P('dp')
- align_weight_grad: float32 [768, 1024], P('dp')
- align_bias_grad: float32 [1024], P('dp')
Inputs may be any that keep to these rules, and one draw needn't show every extreme that they name: `long_length`: 1024 is reached in every draw. `short_length`: 0 marks an empty slot. Entry (s * 2 + r) * 4 + j of a micro-batch's row is home slot j of the device with dp index s and rep index r; a live clip there goes to balanced slot j mod 2 of the device with dp index destination and rep index r. No two live clips meet in one balanced slot, a device sends at most one live clip to any one dp index in a micro-batch, and in every micro-batch some device receives 2 live clips. `destination`: set for empty slots too. `long_index`: the entries of one clip's row are distinct. `short_index`: the entries of one clip's row are distinct.
All inputs are finite; a program needn't handle non-finite values.
Results may differ from a plain program's by a relative error of at most 0.0095.
Values may be sent and summed in bfloat16 or wider, within the bound.
A program may use at most 576 MiB of HBM per device.

v0:
```python
from functools import partial

import jax
import jax.numpy as jnp
from jax import lax
from jax.sharding import PartitionSpec as P

HEADS = 12


EPS = 1e-06
MASKED = -1000000000.0
WEIGHT_NAMES = (
    "position",
    "mixer_gain",
    "mixer_shift",
    "heads_weight",
    "query_bias",
    "value_bias",
    "out_weight",
    "out_bias",
    "dense_gain",
    "dense_shift",
    "up_weight",
    "up_bias",
    "down_weight",
    "down_bias",
    "align_weight",
    "align_bias",
)


def layer_norm(values, gain, shift):
    mean = jnp.mean(values, axis=-1, keepdims=True)
    centered = values - mean
    spread = jnp.mean(centered * centered, axis=-1, keepdims=True)
    return centered * lax.rsqrt(spread + EPS) * gain + shift


def matmul(left, right):
    return jnp.dot(left, right, preferred_element_type=jnp.float32)


def outer_sum(left, right):
    return jnp.einsum("rd,rc->dc", left, right, preferred_element_type=jnp.float32)


def times_transpose(left, right):
    return jnp.einsum("rc,dc->rd", left, right, preferred_element_type=jnp.float32)


def allowed_mask(query_seg, key_seg, key_ok):
    return (query_seg[:, None] == key_seg[None, :]) & key_ok[None, :]


def attend_block(query, keys, values, allowed, scale):
    scores = jnp.einsum("qhe,khe->hqk", query, keys, preferred_element_type=jnp.float32) * scale
    scores = jnp.where(allowed[None], scores, MASKED)
    top = jnp.max(scores, axis=-1, keepdims=True)
    weights = jnp.exp(scores - top)
    total = jnp.sum(weights, axis=-1, keepdims=True)
    probs = (weights / total).astype(jnp.bfloat16)
    output = jnp.einsum("hqk,khe->qhe", probs, values, preferred_element_type=jnp.float32)
    return (output, (top + jnp.log(total))[..., 0])


def attend_back(query, keys, values, grad_out, logsum, allowed, scale):
    scores = jnp.einsum("qhe,khe->hqk", query, keys, preferred_element_type=jnp.float32) * scale
    scores = jnp.where(allowed[None], scores, MASKED)
    probs = jnp.exp(scores - logsum[..., None])
    grad_values = jnp.einsum(
        "hqk,qhe->khe", probs.astype(jnp.bfloat16), grad_out, preferred_element_type=jnp.float32
    )
    grad_probs = jnp.einsum("qhe,khe->hqk", grad_out, values, preferred_element_type=jnp.float32)
    inner = jnp.sum(probs * grad_probs, axis=-1, keepdims=True)
    grad_scores = (probs * (grad_probs - inner)).astype(jnp.bfloat16)
    grad_query = (
        jnp.einsum("hqk,khe->qhe", grad_scores, keys, preferred_element_type=jnp.float32) * scale
    )
    grad_keys = (
        jnp.einsum("hqk,qhe->khe", grad_scores, query, preferred_element_type=jnp.float32) * scale
    )
    return (grad_query, grad_keys, grad_values)


def attention_forward(query, keys, values, regions, scale):
    outputs = []
    sums = []
    for first, count, segment, key_ok, block in regions:
        keys_here = keys[first : first + count]
        values_here = values[first : first + count]
        for begin in range(0, count, block):
            allowed = allowed_mask(segment[begin : begin + block], segment, key_ok)
            output, logsum = attend_block(
                query[first + begin : first + begin + block], keys_here, values_here, allowed, scale
            )
            outputs.append(output)
            sums.append(logsum)
    return (jnp.concatenate(outputs, axis=0), sums)


def attention_backward(query, keys, values, grad_out, sums, regions, scale):
    query_parts = []
    key_parts = []
    value_parts = []
    block_number = 0
    for first, count, segment, key_ok, block in regions:
        keys_here = keys[first : first + count]
        values_here = values[first : first + count]
        key_total = jnp.zeros(keys_here.shape, jnp.float32)
        value_total = jnp.zeros(values_here.shape, jnp.float32)
        for begin in range(0, count, block):
            allowed = allowed_mask(segment[begin : begin + block], segment, key_ok)
            rows_from = first + begin
            grad_query, grad_keys, grad_values = attend_back(
                query[rows_from : rows_from + block],
                keys_here,
                values_here,
                grad_out[rows_from : rows_from + block],
                sums[block_number],
                allowed,
                scale,
            )
            block_number += 1
            query_parts.append(grad_query)
            key_total = key_total + grad_keys
            value_total = value_total + grad_values
        key_parts.append(key_total)
        value_parts.append(value_total)
    return (
        jnp.concatenate(query_parts, axis=0),
        jnp.concatenate(key_parts, axis=0),
        jnp.concatenate(value_parts, axis=0),
    )


def align_back(rows, teach, row_ok, weight, bias):
    projected = matmul(rows, weight) + bias
    grad_proj = jnp.where(row_ok[:, None], projected - teach.astype(jnp.float32), 0.0).astype(
        jnp.bfloat16
    )
    return (
        times_transpose(grad_proj, weight).astype(jnp.bfloat16),
        outer_sum(rows, grad_proj),
        jnp.sum(grad_proj.astype(jnp.float32), axis=0),
    )


def shards(
    long_clips,
    short_clips,
    long_index,
    short_index,
    long_length,
    short_length,
    destination,
    long_target,
    short_target,
    position,
    mixer_gain,
    mixer_shift,
    heads_weight,
    query_bias,
    value_bias,
    out_weight,
    out_bias,
    dense_gain,
    dense_shift,
    up_weight,
    up_bias,
    down_weight,
    down_bias,
    align_weight,
    align_bias,
):
    peers = lax.axis_size("dp")
    copies = lax.axis_size("rep")
    mine = lax.axis_index("dp")
    own_copy = lax.axis_index("rep")
    micros = long_clips.shape[0]
    long_rows = long_clips.shape[2]
    width = long_clips.shape[3]
    home_slots = short_clips.shape[1]
    tile = short_clips.shape[2]
    bal_slots = home_slots // 2
    short_rows = home_slots * tile
    head_dim = width // HEADS
    scale = head_dim ** (-0.5)
    long_block = min(512, long_rows)
    triple_bias = jnp.concatenate([query_bias, jnp.zeros_like(query_bias), value_bias])
    params = (
        position, mixer_gain, mixer_shift, heads_weight, query_bias, value_bias, out_weight, out_bias,
        dense_gain, dense_shift, up_weight, up_bias, down_weight, down_bias, align_weight, align_bias,
    )
    totals = {
        name: jnp.zeros(value.shape, jnp.float32) for name, value in zip(WEIGHT_NAMES, params)
    }
    slot_pick = jnp.arange(home_slots)[:, None] % bal_slots == jnp.arange(bal_slots)[None, :]
    long_seg = jnp.zeros((long_rows,), jnp.int32)
    short_seg = jnp.arange(short_rows) // tile
    long_outs = []
    short_homes = []
    long_grads = []
    short_grads = []
    send_maps = []
    recv_maps = []
    for micro in range(micros):
        group_dest = lax.dynamic_index_in_dim(
            destination[micro].reshape(peers, copies, home_slots), own_copy, 1, keepdims=False
        )
        group_len = lax.dynamic_index_in_dim(
            short_length[micro].reshape(peers, copies, home_slots), own_copy, 1, keepdims=False
        )
        own_dest = lax.dynamic_index_in_dim(group_dest, mine, 0, keepdims=False)
        own_len = lax.dynamic_index_in_dim(group_len, mine, 0, keepdims=False)
        send_maps.append((own_dest[None, :] == jnp.arange(peers)[:, None]) & (own_len[None, :] > 0))
        incoming = (group_dest == mine) & (group_len > 0)
        recv_maps.append(jnp.any(incoming[:, :, None] & slot_pick[None], axis=1))
        stacked = jnp.concatenate(
            [long_clips[micro, 0], short_clips[micro].reshape(short_rows, width)], axis=0
        )
        stacked_index = jnp.concatenate([long_index[micro, 0], short_index[micro].reshape(short_rows)])
        targets = jnp.concatenate(
            [long_target[micro, 0], short_target[micro].reshape(short_rows, -1)], axis=0
        )
        long_ok = jnp.arange(long_rows) < long_length[micro, 0]
        short_ok = (jnp.arange(tile)[None, :] < own_len[:, None]).reshape(short_rows)
        row_ok = jnp.concatenate([long_ok, short_ok])
        regions = (
            (0, long_rows, long_seg, long_ok, long_block),
            (long_rows, short_rows, short_seg, short_ok, short_rows),
        )
        total_rows = stacked.shape[0]
        start = stacked.astype(jnp.float32) + jnp.take(position, stacked_index, axis=0).astype(
            jnp.float32
        )
        mixed, mixer_back = jax.vjp(layer_norm, start, mixer_gain, mixer_shift)
        normed = mixed.astype(jnp.bfloat16)
        triple = (matmul(normed, heads_weight) + triple_bias).astype(jnp.bfloat16)
        query = triple[:, :width].reshape(total_rows, HEADS, head_dim)
        keys_all = triple[:, width : 2 * width].reshape(total_rows, HEADS, head_dim)
        values_all = triple[:, 2 * width :].reshape(total_rows, HEADS, head_dim)
        attended_full, sums = attention_forward(query, keys_all, values_all, regions, scale)
        attended = attended_full.reshape(total_rows, width).astype(jnp.bfloat16)
        middle = start + matmul(attended, out_weight) + out_bias
        dense_full, dense_back = jax.vjp(layer_norm, middle, dense_gain, dense_shift)
        dense = dense_full.astype(jnp.bfloat16)
        upper = matmul(dense, up_weight) + up_bias
        hidden_full, gelu_back = jax.vjp(partial(jax.nn.gelu, approximate=False), upper)
        hidden = hidden_full.astype(jnp.bfloat16)
        result = middle + matmul(hidden, down_weight) + down_bias
        shown = jnp.where(row_ok[:, None], result, 0.0).astype(jnp.bfloat16)
        long_outs.append(shown[:long_rows])
        short_homes.append(shown[long_rows:].reshape(home_slots, tile, width))
        grad_result, weight_term, bias_term = align_back(
            shown, targets, row_ok, align_weight, align_bias
        )
        totals["align_weight"] = totals["align_weight"] + weight_term
        totals["align_bias"] = totals["align_bias"] + bias_term
        totals["down_weight"] = totals["down_weight"] + outer_sum(hidden, grad_result)
        totals["down_bias"] = totals["down_bias"] + jnp.sum(grad_result.astype(jnp.float32), axis=0)
        grad_hidden = times_transpose(grad_result, down_weight)
        grad_upper = gelu_back(grad_hidden)[0].astype(jnp.bfloat16)
        totals["up_weight"] = totals["up_weight"] + outer_sum(dense, grad_upper)
        totals["up_bias"] = totals["up_bias"] + jnp.sum(grad_upper.astype(jnp.float32), axis=0)
        grad_dense = times_transpose(grad_upper, up_weight)
        grad_mid_norm, gain_term, shift_term = dense_back(grad_dense)
        totals["dense_gain"] = totals["dense_gain"] + gain_term
        totals["dense_shift"] = totals["dense_shift"] + shift_term
        grad_middle = grad_result.astype(jnp.float32) + grad_mid_norm
        grad_branch = grad_middle.astype(jnp.bfloat16)
        totals["out_weight"] = totals["out_weight"] + outer_sum(attended, grad_branch)
        totals["out_bias"] = totals["out_bias"] + jnp.sum(grad_branch.astype(jnp.float32), axis=0)
        grad_attended = (
            times_transpose(grad_branch, out_weight)
            .astype(jnp.bfloat16)
            .reshape(total_rows, HEADS, head_dim)
        )
        grad_query, grad_keys, grad_values = attention_backward(
            query, keys_all, values_all, grad_attended, sums, regions, scale
        )
        grad_triple = jnp.concatenate(
            [
                grad_query.reshape(total_rows, width),
                grad_keys.reshape(total_rows, width),
                grad_values.reshape(total_rows, width),
            ],
            axis=1,
        ).astype(jnp.bfloat16)
        totals["heads_weight"] = totals["heads_weight"] + outer_sum(normed, grad_triple)
        triple_sums = jnp.sum(grad_triple.astype(jnp.float32), axis=0)
        totals["query_bias"] = totals["query_bias"] + triple_sums[:width]
        totals["value_bias"] = totals["value_bias"] + triple_sums[2 * width :]
        grad_normed = times_transpose(grad_triple, heads_weight)
        grad_start_norm, gain_term, shift_term = mixer_back(grad_normed)
        totals["mixer_gain"] = totals["mixer_gain"] + gain_term
        totals["mixer_shift"] = totals["mixer_shift"] + shift_term
        grad_start = grad_middle + grad_start_norm
        totals["position"] = totals["position"].at[stacked_index].add(grad_start)
        grad_low = grad_start.astype(jnp.bfloat16)
        long_grads.append(grad_low[:long_rows])
        short_grads.append(grad_low[long_rows:].reshape(home_slots, tile, width))
    send = jnp.stack(
        [
            jnp.einsum("pj,jtd->ptd", m.astype(jnp.bfloat16), h)
            for m, h in zip(send_maps, short_homes)
        ],
        axis=1,
    )
    got = lax.all_to_all(send, "dp", split_axis=0, concat_axis=0, tiled=True)
    short_outs = [
        jnp.einsum("pb,ptd->btd", recv_maps[m].astype(jnp.bfloat16), got[:, m]) for m in range(micros)
    ]
    return (
        jnp.stack(long_outs)[:, None],
        jnp.stack(short_outs),
        jnp.stack(long_grads)[:, None],
        jnp.stack(short_grads),
    ) + combine(totals, copies)


def combine(totals, copies):
    shared = []
    for name in WEIGHT_NAMES:
        total = totals[name]
        if total.ndim == 1:
            shared.append(lax.psum_scatter(lax.psum(total, "rep"), "dp", scatter_dimension=0, tiled=True))
            continue
        peers = lax.axis_size("dp")
        rows = total.shape[0] // peers
        wide = total.astype(jnp.bfloat16)
        padded = -(-rows // (8 * copies)) * 8 * copies
        if padded != rows:
            wide = wide.reshape(peers, rows, -1)
            wide = jnp.pad(wide, ((0, 0), (0, padded - rows), (0, 0)))
            wide = wide.reshape(peers * padded, -1)
        piece = lax.psum_scatter(wide, ("dp", "rep"), scatter_dimension=0, tiled=True)
        piece = lax.all_gather(piece, "rep", axis=0, tiled=True)[:rows]
        shared.append(piece.astype(jnp.float32))
    return tuple(shared)


def solution(mesh):
    placed = (
        P(None, ("dp", "rep"), None, None),
        P(None, ("dp", "rep"), None, None),
        P(None, ("dp", "rep"), None),
        P(None, ("dp", "rep"), None),
        P(None, ("dp", "rep")),
        P(),
        P(),
        P(None, ("dp", "rep"), None, None),
        P(None, ("dp", "rep"), None, None),
        P(),
        P(),
        P(),
        P(),
        P(),
        P(),
        P(),
        P(),
        P(),
        P(),
        P(),
        P(),
        P(),
        P(),
        P(),
        P(),
    )
    return jax.shard_map(
        shards,
        mesh=mesh,
        in_specs=placed,
        out_specs=(
            P(None, ("dp", "rep"), None, None),
            P(None, ("dp", "rep"), None, None),
            P(None, ("dp", "rep"), None, None),
            P(None, ("dp", "rep"), None, None),
            P("dp", None),
            P("dp"),
            P("dp"),
            P("dp", None),
            P("dp"),
            P("dp"),
            P("dp", None),
            P("dp"),
            P("dp"),
            P("dp"),
            P("dp", None),
            P("dp"),
            P("dp", None),
            P("dp"),
            P("dp", None),
            P("dp"),
        ),
        check_vma=False,
    )
```

profile of v0, /device:TPU:0, one launch (start us, length us, event | category | flops | bytes accessed | tf_op | source)
XLA Modules:
  0.0 1399.2 jit_solution(4747551904924863317)
XLA Ops:
  19.2 10.8 gather_fusion
  33.5 10.8 gather_fusion.1
  47.9 6.0 multiply_reduce_fusion.13
  54.6 6.9 fusion.36
  66.4 8.4 fusion.37
  90.0 13.4 fusion.190
  103.4 17.2 %fusion.38 = (f32[12,512]{1,0:T(8,128)}, f32[12,512]{1,0:T(8,128)}, f32[12,512,1024]{2,1,0:T(8,128)}) fusion(pred[1024]{0:T(1024)(128)(4,1)S(1)} %iota_compare_fusion.1, f32[12,512,1024]{2,1,0:T(8,128)} %fusion.190, bf16[512,12,64]{0,2,1:T(8,128)(2,1)} %bitcast.286, bf16[1024,12,64]{0,2,1:T(8,128)(2,1)} %bitcast.265), kind=kOutput, calls=%fused_computation.90 | convolution fusion | flops 843042816 | bytes 52741120 | tf_op jit(solution)/shard_map/qhe,khe->hqk/dot_general | solution.py:57
  120.6 19.2 %fusion = (f32[12,512]{1,0:T(8,128)S(1)}, f32[12,512]{1,0:T(8,128)S(1)}) fusion(f32[12,512]{1,0:T(8,128)} %get-tuple-element.141, f32[12,512,1024]{2,1,0:T(8,128)} %get-tuple-element.256, pred[1024]{0:T(1024)(128)(4,1)S(1)} %iota_compare_fusion.1, f32[12,512]{1,0:T(8,128)} %get-tuple-element.142, f32[12,512,1024]{2,1,0:T(8,128)} %fusion.190), kind=kLoop, calls=%fused_computation.30 | loop fusion | flops 50319360 | bytes 50430976 | tf_op jit(solution)/shard_map/reduce_sum | solution.py:61
  139.9 12.0 fusion.84
  151.9 12.0 fusion.85
  205.6 13.4 fusion.191
  219.0 17.3 %fusion.40 = (f32[12,512]{1,0:T(8,128)}, f32[12,512]{1,0:T(8,128)}, f32[12,512,1024]{2,1,0:T(8,128)}) fusion(pred[1024]{0:T(1024)(128)(4,1)} %iota_compare_fusion, f32[12,512,1024]{2,1,0:T(8,128)} %fusion.191, bf16[512,12,64]{0,2,1:T(8,128)(2,1)} %bitcast.288, bf16[1024,12,64]{0,2,1:T(8,128)(2,1)} %bitcast.269), kind=kOutput, calls=%fused_computation.92 | convolution fusion | flops 843042816 | bytes 52741120 | tf_op jit(solution)/shard_map/qhe,khe->hqk/dot_general | solution.py:57
  236.3 18.8 %fusion.2 = (f32[12,512]{1,0:T(8,128)S(1)}, f32[12,512]{1,0:T(8,128)S(1)}) fusion(f32[12,512]{1,0:T(8,128)} %get-tuple-element.147, f32[12,512,1024]{2,1,0:T(8,128)} %get-tuple-element.253, pred[1024]{0:T(1024)(128)(4,1)} %iota_compare_fusion, f32[12,512]{1,0:T(8,128)} %get-tuple-element.148, f32[12,512,1024]{2,1,0:T(8,128)} %fusion.191), kind=kLoop, calls=%fused_computation.32 | loop fusion | flops 50319360 | bytes 50430976 | tf_op jit(solution)/shard_map/reduce_sum | solution.py:61
  255.2 12.0 fusion.86
  267.2 12.2 fusion.87
  301.3 9.6 fusion.162
  311.0 85.0 %multiply_convert_fusion.5 = (bf16[1280,3072]{1,0:T(8,128)(2,1)S(1)}, f32[1280,3072]{1,0:T(8,128)}, bf16[1280,3072]{1,0:T(8,128)(2,1)}, f32[1280,3072]{1,0:T(8,128)}, f32[1280,3072]{1,0:T(8,128)}) fusion(f32[3072]{0:T(1024)S(1)} %copy-done.226, f32[1280,3072]{1,0:T(8,128)} %fusion.162, bf16[768,3072]{1,0:T(8,128)(2,1)S(1)} %bitcast.361, ...), kind=kOutput, calls=%fused_computation.57 | convolution fusion | flops 6563758080 | bytes 87322624 | tf_op jit(solution)/shard_map/dot_general | solution.py:41
  396.1 6.7 select_convert_fusion.3
  402.8 4.2 convert_reduce_fusion.5
  413.1 6.6 select_convert_fusion.2
  419.8 4.2 convert_reduce_fusion.4
  427.6 23.4 %convert_reduce_fusion = (f32[3072]{0:T(1024)}, bf16[1280,3072]{1,0:T(8,128)(2,1)}) fusion(f32[1280,3072]{1,0:T(8,128)} %get-tuple-element.226, bf16[1280,768]{1,0:T(8,128)(2,1)} %convolution_convert_fusion, bf16[3072,768]{1,0:T(8,128)(2,1)} %param.48, f32[1280,3072]{1,0:T(8,128)} %fusion.162, f32[3072]{0:T(1024)S(1)} %copy-done.227), kind=kOutput, calls=%fused_computation.40 | convolution fusion | flops 6106641408 | bytes 46030848 | tf_op jit(solution)/shard_map/rc,dc->rd/dot_general | solution.py:49
  450.9 11.3 fusion.194
  462.2 21.4 %convert_reduce_fusion.1 = (f32[3072]{0:T(1024)}, bf16[1280,3072]{1,0:T(8,128)(2,1)}) fusion(f32[1280,3072]{1,0:T(8,128)} %get-tuple-element.188, bf16[1280,768]{1,0:T(8,128)(2,1)} %convolution_convert_fusion.1, bf16[3072,768]{1,0:T(8,128)(2,1)} %param.48, f32[1280,3072]{1,0:T(8,128)} %get-tuple-element.261, f32[3072]{0:T(1024)} %param.47), kind=kOutput, calls=%fused_computation.41 | convolution fusion | flops 6106641408 | bytes 46030848 | tf_op jit(solution)/shard_map/rc,dc->rd/dot_general | solution.py:49
  483.8 15.8 %multiply_reduce_fusion.5 = (f32[768]{0:T(1024)}, f32[1280]{0:T(1024)S(1)}, f32[768]{0:T(1024)}, f32[768]{0:T(1024)}, f32[1280]{0:T(1024)S(1)}, /*index=5*/f32[768]{0:T(1024)}, f32[1280,768]{1,0:T(8,128)}) fusion(f32[1280,768]{1,0:T(8,128)} %copy-done.38, f32[1280]{0:T(1024)} %copy-done.171, f32[1280]{0:T(1024)} %copy-done.144, f32[768]{0:T(1024)} %param.44, ...), kind=kOutput, calls=%fused_computation.114 | convolution fusion | flops 6055520256 | bytes 28357632 | tf_op jit(solution)/shard_map/rc,dc->rd/dot_general | solution.py:49
  499.7 5.2 fusion.166
  515.8 4.7 fusion.199
  531.0 10.5 fusion.192
  541.5 37.5 %multiply_reduce_fusion.2 = (f32[12,512]{1,0:T(8,128)}, f32[12,512]{1,0:T(8,128)}, f32[12,512,1024]{2,1,0:T(8,128)}) fusion(f32[12,512]{1,0:T(8,128)} %log_add_fusion.2, f32[12,512,1024]{2,1,0:T(8,128)} %fusion.190, pred[1024]{0:T(1024)(128)(4,1)} %copy-done.189, f32[12,512,1024]{2,1,0:T(8,128)} %fusion.192, f32[12,512]{1,0:T(8,128)} %log_add_fusion.3, ...), kind=kOutput, calls=%fused_computation.11 | convolution fusion | flops 868208640 | bytes 103121920 | tf_op jit(solution)/shard_map/qhe,khe->hqk/dot_general | solution.py:74
  579.1 42.3 %multiply_convert_fusion.2 = (bf16[12,512,1024]{2,1,0:T(8,128)(2,1)}, bf16[12,512,1024]{2,1,0:T(8,128)(2,1)}) fusion(f32[12,512,1024]{2,1,0:T(8,128)} %get-tuple-element.265, f32[12,512]{1,0:T(8,128)} %get-tuple-element.133, f32[12,512]{1,0:T(8,128)} %log_add_fusion.2, f32[12,512,1024]{2,1,0:T(8,128)} %fusion.190, pred[1024]{0:T(1024)(128)(4,1)} %copy-done.189, ...), kind=kLoop, calls=%fused_computation.10 | loop fusion | flops 75497472 | bytes 125928448 | tf_op jit(solution)/shard_map/convert_element_type | solution.py:76
  621.4 9.5 fusion.80
  630.9 8.8 fusion.193
  644.1 12.9 fusion.24
  663.9 10.7 fusion.195
  674.6 37.4 %multiply_reduce_fusion = (f32[12,512]{1,0:T(8,128)}, f32[12,512]{1,0:T(8,128)}, f32[12,512,1024]{2,1,0:T(8,128)}) fusion(f32[12,512]{1,0:T(8,128)} %log_add_fusion, f32[12,512,1024]{2,1,0:T(8,128)} %fusion.191, pred[1024]{0:T(1024)(128)(4,1)} %iota_compare_fusion, f32[12,512,1024]{2,1,0:T(8,128)} %fusion.195, f32[12,512]{1,0:T(8,128)} %log_add_fusion.1, ...), kind=kOutput, calls=%fused_computation.5 | convolution fusion | flops 868208640 | bytes 103121920 | tf_op jit(solution)/shard_map/qhe,khe->hqk/dot_general | solution.py:74
  712.0 42.0 %multiply_convert_fusion = (bf16[12,512,1024]{2,1,0:T(8,128)(2,1)}, bf16[12,512,1024]{2,1,0:T(8,128)(2,1)}) fusion(f32[12,512,1024]{2,1,0:T(8,128)} %get-tuple-element.268, f32[12,512]{1,0:T(8,128)} %get-tuple-element.135, f32[12,512]{1,0:T(8,128)} %log_add_fusion, f32[12,512,1024]{2,1,0:T(8,128)} %fusion.191, pred[1024]{0:T(1024)(128)(4,1)} %iota_compare_fusion, ...), kind=kLoop, calls=%fused_computation.4 | loop fusion | flops 75497472 | bytes 125928448 | tf_op jit(solution)/shard_map/convert_element_type | solution.py:76
  754.0 9.5 fusion.82
  763.5 8.6 fusion.196
  772.2 13.0 fusion.20
  789.0 9.5 fusion.81
  798.5 8.4 fusion.74
  806.9 13.8 fusion.68
  820.7 9.5 fusion.83
  830.3 7.1 fusion.75
  839.0 13.6 fusion.71
  859.6 10.4 fusion.155
  875.0 13.6 add_convert_fusion.4
  888.7 9.5 fusion.198
  898.2 11.9 add_convert_fusion.2
  910.2 11.1 fusion.160
  921.3 12.2 add_convert_fusion.3
  935.5 9.6 fusion.154
  945.2 13.8 multiply_reduce_fusion.7
  960.5 10.7 fusion.165
  971.8 21.0 %scatter_custom_fusion = f32[6272,768]{1,0:T(8,128)} fusion(s32[1280]{0:T(1024)} %fusion.120, f32[]{:T(128)} %constant.202.clone.1, f32[1280,768]{1,0:T(8,128)} %get-tuple-element.176, f32[1280,768]{1,0:T(8,128)} %copy-done.7, bf16[1280,768]{1,0:T(8,128)(2,1)} %convolution_convert_fusion.1, f32[1280]{0:T(1024)} %negate_multiply_fusion.4, ...), kind=kCustom, calls=%fused_computation.94 | custom fusion | flops 5898240 | bytes 29111808 | tf_op jit(solution)/shard_map/scatter-add | solution.py:299
  995.5 26.9 %scatter_custom_fusion.1 = f32[6272,768]{1,0:T(8,128)} fusion(f32[6272,768]{1,0:T(8,128)} %scatter_custom_fusion, s32[1280]{0:T(1024)} %fusion.121, f32[1280,768]{1,0:T(8,128)} %get-tuple-element.232, f32[1280,768]{1,0:T(8,128)} %copy-done.5, bf16[1280,768]{1,0:T(8,128)(2,1)} %convolution_convert_fusion, f32[1280]{0:T(1024)} %negate_multiply_fusion.2, ...), kind=kCustom, calls=%fused_computation.362 | custom fusion | flops 5898240 | bytes 29111296 | tf_op jit(solution)/shard_map/scatter-add | solution.py:299
  1022.4 11.8 convert_element_type.272
  1034.1 8.4 pad.4
  1057.4 8.6 all-to-all-start
  1068.6 5.6 convert_reduce_fusion.7
  1082.2 3.9 convert_reduce_fusion.3
  1086.1 3.9 convert_reduce_fusion.2
  1090.6 111.3 %all-reduce.11 = (f32[768]{0:T(1024)}, f32[768]{0:T(1024)}, f32[768]{0:T(1024)}, f32[768]{0:T(1024)}, f32[768]{0:T(1024)}, /*index=5*/f32[768]{0:T(1024)}, f32[7...) all-reduce(f32[768]{0:T(1024)} %add.473, ...), channel_id=3, replica_groups=mesh['dp'=16,'rep'=2] {'dp'}, use_global_device_ids=true, to_apply=%region_42.44.clone | all-reduce | flops 10240 | bytes 81920
  1255.5 132.9 %reduce-scatter.7.cloned.1.call-done = bf16[200,768]{1,0:T(8,128)(2,1)} async-done(((bf16[6400,768]{1,0:T(8,128)(2,1)}), bf16[200,768]{1,0:T(8,128)(2,1)}) %reduce-scatter.7.cloned.1.call-update) | async-done | bytes 307216 | tf_op jit(solution)/shard_map/reduce_scatter | solution.py:337
  (689 shorter events, 249.8 us)
Async XLA Ops:
  7.2 47.3 %copy-start = (bf16[768,2304]{1,0:T(8,128)(2,1)S(1)}, bf16[768,2304]{1,0:T(8,128)(2,1)}, u32[]{:S(2)}) copy-start(bf16[768,2304]{1,0:T(8,128)(2,1)} %param.39) | copy-start | bytes 10616836
  7.2 1228.2 %reduce-scatter.11.cloned.1.call-start = ((), (), s32[]{:S(2)}) async-start(), calls=%async_computation.9 | async-start | bytes 1216512 | tf_op jit(solution)/shard_map/reduce_scatter | solution.py:337
  19.2 10.8 copy-start.180
  33.5 21.0 %copy-start.146 = (f32[1280]{0:T(1024)}, f32[1280]{0:T(1024)S(1)}, u32[]{:S(2)}) copy-start(f32[1280]{0:T(1024)S(1)} %broadcast_multiply_fusion.3) | copy-start | bytes 15364
  47.8 18.6 %copy-start.149 = (f32[1280]{0:T(1024)}, f32[1280]{0:T(1024)S(1)}, u32[]{:S(2)}) copy-start(f32[1280]{0:T(1024)S(1)} %broadcast_multiply_fusion.1) | copy-start | bytes 15364
  87.4 64.5 %copy-start.189 = (pred[1024]{0:T(1024)(128)(4,1)}, pred[1024]{0:T(1024)(128)(4,1)S(1)}, u32[]{:S(2)}) copy-start(pred[1024]{0:T(1024)(128)(4,1)S(1)} %iota_compare_fusion.1) | copy-start | bytes 3076
  120.6 19.2 %copy-start.30 = (bf16[1024,768]{0,1:T(8,128)(2,1)S(1)}, bf16[1024,768]{0,1:T(8,128)(2,1)}, u32[]{:S(2)}) copy-start(bf16[1024,768]{0,1:T(8,128)(2,1)} %copy.197) | copy-start | bytes 4718596
  120.6 19.2 %copy-start.113 = (f32[12,512]{1,0:T(8,128)S(1)}, f32[12,512]{1,0:T(8,128)}, u32[]{:S(2)}) copy-start(f32[12,512]{1,0:T(8,128)} %get-tuple-element.141) | copy-start | bytes 73732
  139.8 12.1 copy-start.136
  139.8 12.1 copy-start.138
  139.9 12.0 copy-start.115
  151.9 15.9 %copy-start.220 = (s32[2,128]{1,0:T(2,128)S(1)}, s32[2,128]{1,0:T(2,128)}, u32[]{:S(2)}) copy-start(s32[2,128]{1,0:T(2,128)} %param.32) | copy-start | bytes 3076
  169.8 12.5 copy-start.168
  190.0 120.9 %copy-start.144 = (f32[1280]{0:T(1024)}, f32[1280]{0:T(1024)S(1)}, u32[]{:S(2)}) copy-start(f32[1280]{0:T(1024)S(1)} %broadcast_multiply_fusion.2) | copy-start | bytes 15364
  193.1 117.9 %copy-start.171 = (f32[1280]{0:T(1024)}, f32[1280]{0:T(1024)S(1)}, u32[]{:S(2)}) copy-start(f32[1280]{0:T(1024)S(1)} %fusion.117) | copy-start | bytes 15364
  236.3 18.9 %copy-start.32 = (bf16[1024,768]{0,1:T(8,128)(2,1)S(1)}, bf16[1024,768]{0,1:T(8,128)(2,1)}, u32[]{:S(2)}) copy-start(bf16[1024,768]{0,1:T(8,128)(2,1)} %copy.205) | copy-start | bytes 4718596
  236.3 18.9 %copy-start.117 = (f32[12,512]{1,0:T(8,128)S(1)}, f32[12,512]{1,0:T(8,128)}, u32[]{:S(2)}) copy-start(f32[12,512]{1,0:T(8,128)} %get-tuple-element.147) | copy-start | bytes 73732
  236.3 18.9 %copy-start.192 = (pred[1024]{0:T(1024)(128)(4,1)S(1)}, pred[1024]{0:T(1024)(128)(4,1)}, u32[]{:S(2)}) copy-start(pred[1024]{0:T(1024)(128)(4,1)} %iota_compare_fusion) | copy-start | bytes 3076
  255.1 12.1 copy-start.140
  255.1 12.1 copy-start.142
  255.2 12.0 copy-start.119
  288.8 12.5 slice-start
  301.3 9.7 copy-start.39
  311.0 85.0 %copy-start.217 = (pred[1280]{0:T(1024)(128)(4,1)S(1)}, pred[1280]{0:T(1024)(128)(4,1)}, u32[]{:S(2)}) copy-start(pred[1280]{0:T(1024)(128)(4,1)} %pad_add_fusion) | copy-start | bytes 3844
  311.0 85.0 %copy-start.221 = (bf16[3072,768]{1,0:T(8,128)(2,1)S(1)}, bf16[3072,768]{1,0:T(8,128)(2,1)}, u32[]{:S(2)}) copy-start(bf16[3072,768]{1,0:T(8,128)(2,1)} %param.48) | copy-start | bytes 14155780
  311.0 85.0 %copy-start.230 = (f32[768]{0:T(1024)S(1)}, f32[768]{0:T(1024)}, u32[]{:S(2)}) copy-start(f32[768]{0:T(1024)} %param.49) | copy-start | bytes 9220
  462.2 21.4 %copy-start.111 = (f32[1280]{0:T(1024)S(1)}, f32[1280]{0:T(1024)}, u32[]{:S(2)}) copy-start(f32[1280]{0:T(1024)} %copy-done.110) | copy-start | bytes 15364
  462.2 21.4 %copy-start.126 = (f32[1280]{0:T(1024)S(1)}, f32[1280]{0:T(1024)}, u32[]{:S(2)}) copy-start(f32[1280]{0:T(1024)} %copy-done.125) | copy-start | bytes 15364
  483.7 15.9 %copy-start.159 = (f32[1280]{0:T(1024)S(1)}, f32[1280]{0:T(1024)}, u32[]{:S(2)}) copy-start(f32[1280]{0:T(1024)} %copy-done.158) | copy-start | bytes 15364
  483.7 15.9 %copy-start.157 = (f32[1280]{0:T(1024)S(1)}, f32[1280]{0:T(1024)}, u32[]{:S(2)}) copy-start(f32[1280]{0:T(1024)} %copy-done.156) | copy-start | bytes 15364
  483.7 15.9 %copy-start.13 = (f32[1280,768]{1,0:T(8,128)S(1)}, f32[1280,768]{1,0:T(8,128)}, u32[]{:S(2)}) copy-start(f32[1280,768]{1,0:T(8,128)} %copy-done.11) | copy-start | bytes 11796484
  483.7 15.9 %copy-start.40 = (f32[1280,768]{1,0:T(8,128)S(1)}, f32[1280,768]{1,0:T(8,128)}, u32[]{:S(2)}) copy-start(f32[1280,768]{1,0:T(8,128)} %copy-done.38) | copy-start | bytes 11796484
  483.7 15.9 %copy-start.68 = (f32[1280,768]{1,0:T(8,128)S(1)}, f32[1280,768]{1,0:T(8,128)}, u32[]{:S(2)}) copy-start(f32[1280,768]{1,0:T(8,128)} %fusion.194) | copy-start | bytes 11796484
  483.7 15.9 %copy-start.145 = (f32[1280]{0:T(1024)S(1)}, f32[1280]{0:T(1024)}, u32[]{:S(2)}) copy-start(f32[1280]{0:T(1024)} %copy-done.144) | copy-start | bytes 15364
  483.7 15.9 %copy-start.162 = (f32[768]{0:T(1024)S(1)}, f32[768]{0:T(1024)}, u32[]{:S(2)}) copy-start(f32[768]{0:T(1024)} %param.44) | copy-start | bytes 9220
  483.8 15.9 %copy-start.172 = (f32[1280]{0:T(1024)S(1)}, f32[1280]{0:T(1024)}, u32[]{:S(2)}) copy-start(f32[1280]{0:T(1024)} %copy-done.171) | copy-start | bytes 15364
  515.7 722.4 %reduce-scatter.17.cloned.1.call-start = ((), (), s32[]{:S(2)}) async-start(), calls=%async_computation.12 | async-start | bytes 1622016 | tf_op jit(solution)/shard_map/reduce_scatter | solution.py:337
  524.1 716.8 %reduce-scatter.9.cloned.1.call-start = ((), (), s32[]{:S(2)}) async-start(), calls=%async_computation.8 | async-start | bytes 3649536 | tf_op jit(solution)/shard_map/reduce_scatter | solution.py:337
  530.1 11.4 copy-start.57
  579.0 42.3 %copy-start.8 = (bf16[1024,768]{0,1:T(8,128)(2,1)S(1)}, bf16[1024,768]{0,1:T(8,128)(2,1)}, u32[]{:S(2)}) copy-start(bf16[1024,768]{0,1:T(8,128)(2,1)} %copy.199) | copy-start | bytes 4718596
  663.0 11.6 copy-start.59
  712.0 42.0 %copy-start.10 = (bf16[1024,768]{0,1:T(8,128)(2,1)S(1)}, bf16[1024,768]{0,1:T(8,128)(2,1)}, u32[]{:S(2)}) copy-start(bf16[1024,768]{0,1:T(8,128)(2,1)} %copy.207) | copy-start | bytes 4718596
  772.1 13.0 copy-start.2
  772.1 13.0 copy-start.74
  772.1 13.0 copy-start.95
  839.0 13.7 copy-start.43
  839.0 13.7 copy-start.100
  859.6 10.4 copy-start.71
  888.7 360.7 %reduce-scatter.15.cloned.1.call-start = ((), (), s32[]{:S(2)}) async-start(), calls=%async_computation.11 | async-start | bytes 4866048 | tf_op jit(solution)/shard_map/reduce_scatter | solution.py:337
  910.1 11.2 copy-start.112
  910.1 11.2 copy-start.127
  910.1 342.3 %reduce-scatter.13.cloned.1.call-start = ((), (), s32[]{:S(2)}) async-start(), calls=%async_computation.10 | async-start | bytes 4866048 | tf_op jit(solution)/shard_map/reduce_scatter | solution.py:337
  910.2 11.2 copy-start.14
  910.2 11.2 copy-start.163
  910.2 11.2 copy-start.170
  933.5 454.9 %reduce-scatter.7.cloned.1.call-start = ((), (), s32[]{:S(2)}) async-start(), calls=%async_computation.7 | async-start | bytes 10137600 | tf_op jit(solution)/shard_map/reduce_scatter | solution.py:337
  935.5 9.7 copy-start.151
  935.5 9.7 copy-start.175
  935.5 9.7 copy-start.178
  945.2 13.9 copy-start.155
  945.2 14.6 %copy-start.153 = (f32[1280]{0:T(1024)S(1)}, f32[1280]{0:T(1024)}, u32[]{:S(2)}) copy-start(f32[1280]{0:T(1024)} %copy-done.152) | copy-start | bytes 15364
  960.5 11.3 copy-start.135
  971.8 23.7 %copy-start.133 = (f32[1280]{0:T(1024)S(1)}, f32[1280]{0:T(1024)}, u32[]{:S(2)}) copy-start(f32[1280]{0:T(1024)} %copy-done.132) | copy-start | bytes 15364
  1057.4 186.5 %all-to-all-start = ((bf16[16,2,64,768]{3,2,1,0:T(8,128)(2,1)}), bf16[16,2,64,768]{3,2,1,0:T(8,128)(2,1)}, u32[]{:S(2)}, u32[]{:S(2)}) async-start(bf16[16,2,64,768]{3,2,1,0:T(8,128)(2,1)} %copy.217), calls=%async_computation | async-start | bytes 6291456 | tf_op jit(solution)/shard_map/all_to_all | solution.py:310
  (183 other events, 824.4 us)
Sparse Core Ops, SparseCore 0:
  515.8 98.9 reduce-scatter.10
  620.1 96.1 reduce-scatter.16
  888.8 105.9 reduce-scatter.8
  1000.1 135.1 reduce-scatter.14
  1141.5 104.3 reduce-scatter.12
  1251.7 136.6 reduce-scatter.6
where the time goes:
time: 1410 us; the launch traced here: 1400 us
  matrix products  675 us (48%)
  other arithmetic  278 us (20%)
  local copies, waits for them, and re-layouts  157 us (11%)
  waiting for transfers between devices  133 us (9%)
  blocking collectives  128 us (9%)
  between operations  19.1 us (1%)
    dot_general x10, matrix products, matmul(): return jnp.dot(left, right, preferred_element_type=jnp.float32)  136 us
    reduce_scatter x6, waiting for transfers between devices, combine(): lax.psum_scatter(wide, ('dp', 'rep'), scatter_dimension=0, tiled=True)  133 us
    unnamed x1, blocking collectives  111 us
    dot_general x10, matrix products, times_transpose(): jnp.einsum('rc,dc->rd', left, right, preferred_element_type=jnp.float32)  108 us
    dot_general x6, matrix products, attend_back(): jnp.einsum('qhe,khe->hqk', grad_out, values, preferred_element_type=jnp.f...  99.4 us
    convert_element_type x4, other arithmetic, attend_back(): grad_scores = (probs * (grad_probs - inner)).astype(jnp.bfloat16)  85.9 us
    dot_general x10, matrix products, outer_sum(): jnp.einsum('rd,rc->dc', left, right, preferred_element_type=jnp.float32)  81.2 us
    dot_general x6, matrix products, attend_block(): jnp.einsum('qhe,khe->hqk', query, keys, preferred_element_type=jnp.float32)  64.9 us
  transfers between devices with their start and end apart: 7, of which 1 were waited for; matrix products, arithmetic and copies ran while one was open for 42% of the time, Pallas kernels for 0%

commit v1 on v0

v1 whole, which is shorter than its diff:
```python
from functools import partial

import jax
import jax.numpy as jnp
from jax import lax
from jax.experimental import pallas as pl
from jax.experimental.pallas import tpu as pltpu
from jax.sharding import PartitionSpec as P

HEADS = 12
EPS = 1e-06
MASKED = -1000000000.0
WEIGHT_NAMES = (
    "position",
    "mixer_gain",
    "mixer_shift",
    "heads_weight",
    "query_bias",
    "value_bias",
    "out_weight",
    "out_bias",
    "dense_gain",
    "dense_shift",
    "up_weight",
    "up_bias",
    "down_weight",
    "down_bias",
    "align_weight",
    "align_bias",
)


BLOCK = 256
BF = jnp.bfloat16
F32 = jnp.float32
VMEM_LIMIT = 66_000_000


def dot(left, right, dims):
    return lax.dot_general(left, right, ((dims[:1], dims[1:]), ((), ())), preferred_element_type=F32)


def centre(values):
    mean = jnp.mean(values, axis=-1, keepdims=True)
    centered = values - mean
    spread = jnp.mean(centered * centered, axis=-1, keepdims=True)
    inverse = lax.rsqrt(spread + EPS)
    return centered * inverse, inverse


def centre_back(grad, unit, inverse):
    first = jnp.mean(grad, axis=-1, keepdims=True)
    second = jnp.mean(grad * unit, axis=-1, keepdims=True)
    return inverse * (grad - first - unit * second)


def valid_rows(tile_len, block, tile):
    row = lax.broadcasted_iota(jnp.int32, (BLOCK, 1), 0)
    parts = BLOCK // tile
    limit = tile_len[block * parts]
    for part in range(1, parts):
        limit = jnp.where(row >= part * tile, tile_len[block * parts + part], limit)
    return lax.rem(row, tile) < limit


def live_block(tile_len, block, tile):
    most = tile_len[block * (BLOCK // tile)]
    for part in range(1, BLOCK // tile):
        most = jnp.maximum(most, tile_len[block * (BLOCK // tile) + part])
    return most > 0


def project_kernel(
    tile, tile_len, held, source, index, *refs
):
    parts = BLOCK // tile
    pieces = refs[:parts]
    table_any, weight, bias, gain, shift, out, start_out, table, stage, rows, sem = refs[parts:]
    step = pl.program_id(0)
    width = weight.shape[0]
    chunk = stage.shape[1]
    chunks = table.shape[0] // chunk

    def fetch(number):
        return pltpu.make_async_copy(
            table_any.at[pl.ds(pl.multiple_of(number * chunk, 16), chunk), :],
            stage.at[lax.rem(number, 2)],
            sem.at[lax.rem(number, 2)],
        )

    @pl.when(step == 0)
    def _():
        fetch(0).start()

        def load(number, carry):
            @pl.when(number + 1 < chunks)
            def _():
                fetch(number + 1).start()

            fetch(number).wait()
            table[pl.ds(pl.multiple_of(number * chunk, 16), chunk), :] = stage[lax.rem(number, 2)].astype(F32)
            return carry

        lax.fori_loop(0, chunks, load, 0)

    @pl.when(live_block(tile_len, step, tile))
    def _():
        def gather(group, carry):
            base = pl.multiple_of(group * 8, 8)
            for row in range(8):
                place = index[step * BLOCK + base + row]
                rows[pl.ds(base + row, 1), :] = table[pl.ds(place, 1), :]
            return carry

        lax.fori_loop(0, BLOCK // 8, gather, 0)
        whole = jnp.concatenate([piece[...] for piece in pieces], axis=0).astype(F32)
        start = whole + rows[...]
        start_out[...] = start
        unit, _ = centre(start)
        normed = (unit * gain[...] + shift[...]).astype(BF)
        for part in range(3):
            cols = slice(part * width, (part + 1) * width)
            triple = (dot(normed, weight[:, cols], (1, 0)) + bias[:, cols]).astype(BF)
            if part == 0:
                triple = triple * BF(0.125)
            out[cols, :] = triple.T


def masked_tile(tile_scores, limit):
    key = lax.broadcasted_iota(jnp.int32, tile_scores.shape, 0)
    return jnp.where(key < limit, tile_scores, MASKED)


def block_mask(tile_len, first, tile):
    key = lax.broadcasted_iota(jnp.int32, (BLOCK, BLOCK), 0)
    asked = lax.broadcasted_iota(jnp.int32, (BLOCK, BLOCK), 1)
    limit = tile_len[first]
    for part in range(1, BLOCK // tile):
        limit = jnp.where(key >= part * tile, tile_len[first + part], limit)
    return (key // tile == asked // tile) & (lax.rem(key, tile) < limit)


def attend_kernel(tile, long_rows, clips, tile_len, length, count, query, keys, values, out, logsum):
    head_dim = query.shape[0] // 2
    most = long_rows // BLOCK

    def one(column, first, size, fix):
        for head in range(2):
            lanes = slice(head * head_dim, (head + 1) * head_dim)
            asked = query[lanes, pl.ds(column, BLOCK)]
            scores = []
            for number in range(size):
                held = keys[lanes, pl.ds(first + number * BLOCK, BLOCK)]
                scores.append(dot(held, asked, (0, 0)))
            scores[-1] = fix(scores[-1])
            top = jnp.max(scores[0], axis=0, keepdims=True)
            for score in scores[1:]:
                top = jnp.maximum(top, jnp.max(score, axis=0, keepdims=True))
            weights = [jnp.exp(score - top) for score in scores]
            total = sum(jnp.sum(weight, axis=0, keepdims=True) for weight in weights)
            gathered = None
            for number, weight in enumerate(weights):
                held = values[lanes, pl.ds(first + number * BLOCK, BLOCK)]
                term = dot(held, weight.astype(BF), (1, 0))
                gathered = term if gathered is None else gathered + term
            out[lanes, pl.ds(column, BLOCK)] = (gathered / total).astype(BF)
            logsum[0, pl.ds(head, 1), pl.ds(column, BLOCK)] = top + jnp.log(total)

    def clip(number, carry):
        first = pl.multiple_of(number * long_rows, BLOCK)
        blocks = count[number]
        rest = length[number]
        for size in range(1, most + 1):
            @pl.when(blocks == size)
            def _():
                def ask(block, inner):
                    one(
                        pl.multiple_of(first + block * BLOCK, BLOCK),
                        first,
                        size,
                        lambda score: masked_tile(score, rest - (size - 1) * BLOCK),
                    )
                    return inner

                lax.fori_loop(0, size, ask, 0)
        return carry

    lax.fori_loop(0, clips, clip, 0)

    def short(number, carry):
        column = pl.multiple_of(clips * long_rows + number * BLOCK, BLOCK)
        allowed = block_mask(tile_len, (clips * long_rows + number * BLOCK) // tile, tile)
        one(column, column, 1, lambda score: jnp.where(allowed, score, MASKED))
        return carry

    lax.fori_loop(0, count[clips], short, 0)


def attend_back_kernel(
    tile, long_rows, clips, tile_len, length, count, query, keys, values, grad, logsum,
    query_out, key_out, value_out, key_sum, value_sum,
):
    head_dim = query.shape[0] // 2
    most = long_rows // BLOCK

    def one(column, first, size, fix):
        for head in range(2):
            lanes = slice(head * head_dim, (head + 1) * head_dim)
            asked = query[lanes, pl.ds(column, BLOCK)]
            pulled = grad[lanes, pl.ds(column, BLOCK)]
            base = logsum[0, pl.ds(head, 1), pl.ds(column, BLOCK)]
            probs = []
            terms = []
            inner = None
            for number in range(size):
                here = pl.ds(first + number * BLOCK, BLOCK)
                score = dot(keys[lanes, here], asked, (0, 0))
                if number == size - 1:
                    score = fix(score)
                prob = jnp.exp(score - base)
                back = dot(values[lanes, here], pulled, (0, 0))
                term = prob * back
                part = jnp.sum(term, axis=0, keepdims=True)
                inner = part if inner is None else inner + part
                probs.append(prob)
                terms.append(term)
            query_sum = None
            for number in range(size):
                here = pl.ds(first + number * BLOCK, BLOCK)
                there = slice(number * BLOCK, (number + 1) * BLOCK)
                moved = (terms[number] - probs[number] * inner).astype(BF)
                value_sum[lanes, there] += dot(pulled, probs[number].astype(BF), (1, 1))
                key_sum[lanes, there] += dot(asked, moved, (1, 1))
                term = dot(keys[lanes, here], moved, (1, 0))
                query_sum = term if query_sum is None else query_sum + term
            query_out[lanes, pl.ds(column, BLOCK)] = (query_sum * 0.125).astype(BF)

    def flush(first, size):
        key_out[:, pl.ds(first, size * BLOCK)] = key_sum[:, : size * BLOCK].astype(BF)
        value_out[:, pl.ds(first, size * BLOCK)] = value_sum[:, : size * BLOCK].astype(BF)

    def clear(size):
        key_sum[:, : size * BLOCK] = jnp.zeros((2 * head_dim, size * BLOCK), F32)
        value_sum[:, : size * BLOCK] = jnp.zeros((2 * head_dim, size * BLOCK), F32)

    def clip(number, carry):
        first = pl.multiple_of(number * long_rows, BLOCK)
        blocks = count[number]
        rest = length[number]
        for size in range(1, most + 1):
            @pl.when(blocks == size)
            def _():
                clear(size)

                def ask(block, inner):
                    one(
                        pl.multiple_of(first + block * BLOCK, BLOCK),
                        first,
                        size,
                        lambda score: masked_tile(score, rest - (size - 1) * BLOCK),
                    )
                    return inner

                lax.fori_loop(0, size, ask, 0)
                flush(first, size)
        return carry

    lax.fori_loop(0, clips, clip, 0)

    def short(number, carry):
        column = pl.multiple_of(clips * long_rows + number * BLOCK, BLOCK)
        allowed = block_mask(tile_len, (clips * long_rows + number * BLOCK) // tile, tile)
        clear(1)
        one(column, column, 1, lambda score: jnp.where(allowed, score, MASKED))
        flush(column, 1)
        return carry

    lax.fori_loop(0, count[clips], short, 0)


def gelu_both(upper):
    spread = 0.5 * (1.0 + lax.erf(upper * 0.7071067811865476))
    bell = jnp.exp(-0.5 * upper * upper) * 0.3989422804014327
    return upper * spread, spread + upper * bell


def write_out(pairs, stage, sem):
    waiting = [None, None]
    for number, (source, target) in enumerate(pairs):
        slot = number % 2
        if waiting[slot] is not None:
            waiting[slot].wait()
        value = source()
        view = stage.at[slot, :, : value.shape[1]]
        stage[slot, :, : value.shape[1]] = value.astype(BF)
        copy = pltpu.make_async_copy(view, target, sem.at[slot])
        copy.start()
        waiting[slot] = copy
    for copy in waiting:
        if copy is not None:
            copy.wait()


def middle_kernel(tile, long_blocks, tile_len, held, source, attended_t, start_in, *refs):
    parts = BLOCK // tile
    targets = refs[:parts]
    (
        out_w, out_b, gain, shift, up_w, up_b, down_w, down_b, align_w, align_b,
        long_out, short_out, pull_out, grad_out, vector_out,
        out_g, up_g, down_g, align_g,
        out_acc, up_acc, down_acc, align_acc, hidden, slope, stage, sem,
    ) = refs[parts:]
    step = pl.program_id(0)
    width = out_w.shape[0]
    wide = up_w.shape[1]
    teach = align_w.shape[1]
    pieces = wide // width
    live = live_block(tile_len, step, tile)

    @pl.when(step == 0)
    def _():
        for acc in (out_acc, up_acc, down_acc, align_acc):
            acc[...] = jnp.zeros_like(acc)
        vector_out[...] = jnp.zeros_like(vector_out)

    def put(value):
        @pl.when(step < long_blocks)
        def _():
            long_out[...] = value

        @pl.when(step >= long_blocks)
        def _():
            short_out[...] = value

    def add_vector(row, value):
        size = value.shape[1]
        vector_out[row : row + 1, :size] += value

    def over_rows(value):
        return jnp.sum(value, axis=0, keepdims=True)

    @pl.when(jnp.logical_not(live))
    def _():
        put(jnp.zeros((BLOCK, width), BF))

    @pl.when(live)
    def _():
        ok = valid_rows(tile_len, step, tile)
        across = attended_t[...]
        middle = start_in[...] + dot(across, out_w[...], (0, 0)) + out_b[...]
        unit, inverse = centre(middle)
        dense = (unit * gain[...] + shift[...]).astype(BF)
        result = middle + down_b[...]
        for piece in range(pieces):
            cols = slice(piece * width, (piece + 1) * width)
            upper = dot(dense, up_w[:, cols], (1, 0)) + up_b[:, cols]
            bent, tilt = gelu_both(upper)
            low = bent.astype(BF)
            hidden[:, cols] = low
            slope[:, cols] = tilt
            result = result + dot(low, down_w[cols, :], (1, 0))
        shown = jnp.where(ok, result, 0.0).astype(BF)
        put(shown)
        projected = dot(shown, align_w[...], (1, 0)) + align_b[...]
        target = jnp.concatenate([piece[...] for piece in targets], axis=0).astype(F32)
        miss = jnp.where(ok, projected - target, 0.0).astype(BF)
        add_vector(5, over_rows(miss.astype(F32)))
        align_acc[...] += dot(shown, miss, (0, 0))
        pulled = dot(miss, align_w[...], (1, 1)).astype(BF)
        pulled_wide = pulled.astype(F32)
        add_vector(4, over_rows(pulled_wide))
        grad_dense = None
        for piece in range(pieces):
            cols = slice(piece * width, (piece + 1) * width)
            grad_upper = dot(pulled, down_w[cols, :], (1, 1)) * slope[:, cols]
            low = grad_upper.astype(BF)
            vector_out[0:1, cols] += over_rows(low.astype(F32))
            down_acc[piece] += dot(hidden[:, cols], pulled, (0, 0))
            up_acc[piece] += dot(dense, low, (0, 0))
            term = dot(low, up_w[:, cols], (1, 1))
            grad_dense = term if grad_dense is None else grad_dense + term
        add_vector(2, over_rows(grad_dense * unit))
        add_vector(3, over_rows(grad_dense))
        grad_middle = pulled_wide + centre_back(grad_dense * gain[...], unit, inverse)
        grad_out[...] = grad_middle
        branch = grad_middle.astype(BF)
        add_vector(1, over_rows(branch.astype(F32)))
        out_acc[...] += dot(across, branch, (1, 0))
        pull_out[...] = dot(out_w[...], branch, (1, 1)).astype(BF)

    @pl.when(step == pl.num_programs(0) - 1)
    def _():
        pairs = [(lambda: out_acc[...], out_g)]
        for piece in range(pieces):
            cols = pl.ds(piece * width, width)
            pairs.append((lambda piece=piece: up_acc[piece], up_g.at[:, cols]))
            pairs.append((lambda piece=piece: down_acc[piece], down_g.at[cols, :]))
        for begin in range(0, teach, width):
            end = min(teach, begin + width)
            pairs.append(
                (lambda begin=begin, end=end: align_acc[:, begin:end], align_g.at[:, pl.ds(begin, end - begin)])
            )
        write_out(pairs, stage, sem)


def entry_kernel(tile, long_blocks, tile_len, held, index, *refs):
    (
        query_t, key_t, value_t, start_in, grad_in, weight, gain, shift,
        long_out, short_out, vector_out, weight_g, position_g,
        weight_acc, position_acc, moved, stage, sem,
    ) = refs
    step = pl.program_id(0)
    width = weight.shape[0]
    live = live_block(tile_len, step, tile)

    @pl.when(step == 0)
    def _():
        weight_acc[...] = jnp.zeros_like(weight_acc)
        vector_out[...] = jnp.zeros_like(vector_out)

        def clear(number, carry):
            position_acc[pl.ds(pl.multiple_of(number * 64, 64), 64), :] = jnp.zeros((64, width), F32)
            return carry

        lax.fori_loop(0, position_acc.shape[0] // 64, clear, 0)

    def put(value):
        @pl.when(step < long_blocks)
        def _():
            long_out[...] = value

        @pl.when(step >= long_blocks)
        def _():
            short_out[...] = value

    def over_rows(value):
        return jnp.sum(value, axis=0, keepdims=True)

    @pl.when(jnp.logical_not(live))
    def _():
        put(jnp.zeros((BLOCK, width), BF))

    @pl.when(live)
    def _():
        unit, inverse = centre(start_in[...])
        normed = (unit * gain[...] + shift[...]).astype(BF)
        grad_normed = None
        for part in range(3):
            cols = slice(part * width, (part + 1) * width)
            across = (query_t, key_t, value_t)[part][...]
            if part != 1:
                vector_out[part : part + 1, :] += over_rows(across.T.astype(F32))
            weight_acc[:, cols] += dot(normed, across, (0, 1))
            term = dot(across, weight[:, cols], (0, 1))
            grad_normed = term if grad_normed is None else grad_normed + term
        vector_out[1:2, :] += over_rows(grad_normed * unit)
        vector_out[3:4, :] += over_rows(grad_normed)
        grad_start = grad_in[...] + centre_back(grad_normed * gain[...], unit, inverse)
        put(grad_start.astype(BF))
        moved[...] = grad_start
        parts = BLOCK // tile

        def spread(number, carry):
            first = number * tile

            def some(group, inner):
                base = pl.multiple_of(first + group * 8, 8)
                for row in range(8):
                    place = index[step * BLOCK + base + row]
                    position_acc[pl.ds(place, 1), :] += moved[pl.ds(base + row, 1), :]
                return inner

            groups = (tile_len[step * parts + number] + 7) // 8
            lax.fori_loop(0, groups, some, 0)
            return carry

        lax.fori_loop(0, parts, spread, 0)

    @pl.when(step == pl.num_programs(0) - 1)
    def _():
        pairs = []
        for part in range(3):
            cols = slice(part * width, (part + 1) * width)
            pairs.append((lambda cols=cols: weight_acc[:, cols], weight_g.at[:, pl.ds(part * width, width)]))
        write_out(pairs, stage, sem)
        chunk = 448

        def copy(number):
            return pltpu.make_async_copy(
                stage.at[lax.rem(number, 2), pl.ds(0, chunk), :],
                position_g.at[pl.ds(pl.multiple_of(number * chunk, 16), chunk), :],
                sem.at[lax.rem(number, 2)],
            )

        def drain(number, carry):
            @pl.when(number >= 2)
            def _():
                copy(number - 2).wait()

            stage[lax.rem(number, 2), pl.ds(0, chunk), :] = position_acc[
                pl.ds(pl.multiple_of(number * chunk, 16), chunk), :
            ].astype(BF)
            copy(number).start()
            return carry

        chunks = position_acc.shape[0] // chunk
        lax.fori_loop(0, chunks, drain, 0)
        copy(chunks - 2).wait()
        copy(chunks - 1).wait()


def whole(shape):
    return pl.BlockSpec(shape, lambda *_: (0,) * len(shape), pipeline_mode=pl.Buffered(1))


def plan_rows(lengths, short_len, tile, long_rows):
    micros = lengths.shape[0]
    per = long_rows // tile
    starts = jnp.arange(per) * tile
    long_tiles = jnp.clip(lengths[:, None] - starts[None, :], 0, tile).reshape(-1)
    slots = short_len.shape[0]
    live = short_len > 0
    before = jnp.arange(slots)[None, :] < jnp.arange(slots)[:, None]
    rank_live = jnp.sum(jnp.where(before & live[None, :], 1, 0), axis=1)
    rank_dead = jnp.sum(jnp.where(before & ~live[None, :], 1, 0), axis=1)
    total = jnp.sum(live.astype(jnp.int32))
    rank = jnp.where(live, rank_live, total + rank_dead)
    chosen = rank[None, :] == jnp.arange(slots)[:, None]
    order = jnp.sum(jnp.where(chosen, jnp.arange(slots)[None, :], 0), axis=1)
    packed_len = jnp.sum(jnp.where(chosen, short_len[None, :], 0), axis=1)
    tile_len = jnp.concatenate([long_tiles, packed_len]).astype(jnp.int32)
    source = jnp.concatenate([jnp.arange(micros * per), micros * per + order]).astype(jnp.int32)
    parts = BLOCK // tile
    blocks = tile_len.shape[0] // parts
    active = jnp.max(tile_len.reshape(blocks, parts), axis=1) > 0
    ids = jnp.arange(blocks)
    held = jnp.max(jnp.where((ids[None, :] <= ids[:, None]) & active[None, :], ids[None, :], 0), axis=1)
    count = jnp.concatenate([-(-lengths // BLOCK), -(-total[None] // parts)]).astype(jnp.int32)
    return tile_len, source, held.astype(jnp.int32), count, chosen


def run_block(
    rows, index, targets, tile_len, source, held, count, lengths, tile, long_rows, micros, weights
):
    w = weights
    total, width = rows.shape
    wide = w["up_weight"].shape[1]
    teach = targets.shape[1]
    patches = w["position"].shape[0]
    blocks = total // BLOCK
    parts = BLOCK // tile
    long_blocks = micros * long_rows // BLOCK
    short_total = total - micros * long_rows
    pairs = HEADS // 2
    pair = width // pairs
    lane = lambda name: w[name].reshape(1, -1)
    params = lambda **more: pltpu.CompilerParams(vmem_limit_bytes=VMEM_LIMIT, **more)
    tiles = lambda last: [
        pl.BlockSpec((tile, last), lambda i, tl, hd, src, *_, part=part: (src[hd[i] * parts + part], 0))
        for part in range(parts)
    ]
    by_block = lambda last: pl.BlockSpec((BLOCK, last), lambda i, tl, hd, *_: (hd[i], 0))
    by_column = lambda first: pl.BlockSpec((first, BLOCK), lambda i, tl, hd, *_: (0, hd[i]))
    long_spec = pl.BlockSpec((BLOCK, width), lambda i, *_: (jnp.minimum(i, long_blocks - 1), 0))
    short_spec = pl.BlockSpec((BLOCK, width), lambda i, *_: (jnp.maximum(i - long_blocks, 0), 0))
    anywhere = pl.BlockSpec(memory_space=pl.ANY)
    bias = jnp.concatenate([w["query_bias"], jnp.zeros_like(w["query_bias"]), w["value_bias"]]).reshape(1, -1)

    triple_t, start = pl.pallas_call(
        partial(project_kernel, tile),
        grid_spec=pltpu.PrefetchScalarGridSpec(
            num_scalar_prefetch=4,
            grid=(blocks,),
            in_specs=tiles(width)
            + [anywhere, whole((width, 3 * width)), whole((1, 3 * width)), whole((1, width)), whole((1, width))],
            out_specs=[by_column(3 * width), by_block(width)],
            scratch_shapes=[
                pltpu.VMEM((patches, width), F32),
                pltpu.VMEM((2, 448, width), BF),
                pltpu.VMEM((BLOCK, width), F32),
                pltpu.SemaphoreType.DMA((2,)),
            ],
        ),
        out_shape=[
            jax.ShapeDtypeStruct((3 * width, total), BF),
            jax.ShapeDtypeStruct((total, width), F32),
        ],
        compiler_params=params(),
        name="project",
    )(
        tile_len, held, source, index, *([rows] * parts), w["position"], w["heads_weight"], bias,
        lane("mixer_gain"), lane("mixer_shift"),
    )

    def heads_spec(offset):
        return pl.BlockSpec((pair, total), lambda i, *_: (i + offset * pairs, 0))

    sums_spec = pl.BlockSpec((1, 2, total), lambda i, *_: (i, 0, 0))
    attended_t, sums = pl.pallas_call(
        partial(attend_kernel, tile, long_rows, micros),
        grid_spec=pltpu.PrefetchScalarGridSpec(
            num_scalar_prefetch=3,
            grid=(pairs,),
            in_specs=[heads_spec(0), heads_spec(1), heads_spec(2)],
            out_specs=[heads_spec(0), sums_spec],
        ),
        out_shape=[
            jax.ShapeDtypeStruct((width, total), BF),
            jax.ShapeDtypeStruct((pairs, 2, total), F32),
        ],
        compiler_params=params(),
        name="attend",
    )(tile_len, lengths, count, triple_t, triple_t, triple_t)

    middle_out = pl.pallas_call(
        partial(middle_kernel, tile, long_blocks),
        grid_spec=pltpu.PrefetchScalarGridSpec(
            num_scalar_prefetch=3,
            grid=(blocks,),
            in_specs=[by_column(width), by_block(width)]
            + tiles(teach)
            + [
                whole((width, width)), whole((1, width)), whole((1, width)), whole((1, width)),
                whole((width, wide)), whole((1, wide)), whole((wide, width)), whole((1, width)),
                whole((width, teach)), whole((1, teach)),
            ],
            out_specs=[
                long_spec, short_spec, by_column(width), by_block(width), whole((8, wide)),
                anywhere, anywhere, anywhere, anywhere,
            ],
            scratch_shapes=[
                pltpu.VMEM((width, width), F32),
                pltpu.VMEM((wide // width, width, width), F32),
                pltpu.VMEM((wide // width, width, width), F32),
                pltpu.VMEM((width, teach), F32),
                pltpu.VMEM((BLOCK, wide), BF),
                pltpu.VMEM((BLOCK, wide), F32),
                pltpu.VMEM((2, width, width), BF),
                pltpu.SemaphoreType.DMA((2,)),
            ],
        ),
        out_shape=[
            jax.ShapeDtypeStruct((micros * long_rows, width), BF),
            jax.ShapeDtypeStruct((short_total, width), BF),
            jax.ShapeDtypeStruct((width, total), BF),
            jax.ShapeDtypeStruct((total, width), F32),
            jax.ShapeDtypeStruct((8, wide), F32),
            jax.ShapeDtypeStruct((width, width), BF),
            jax.ShapeDtypeStruct((width, wide), BF),
            jax.ShapeDtypeStruct((wide, width), BF),
            jax.ShapeDtypeStruct((width, teach), BF),
        ],
        compiler_params=params(),
        name="middle",
    )(
        tile_len, held, source, attended_t, start, *([targets] * parts),
        w["out_weight"], lane("out_bias"), lane("dense_gain"), lane("dense_shift"),
        w["up_weight"], lane("up_bias"), w["down_weight"], lane("down_bias"),
        w["align_weight"], lane("align_bias"),
    )
    long_out, short_out, pulled_t, grad_middle, vector, out_g, up_g, down_g, align_g = middle_out

    grads = pl.pallas_call(
        partial(attend_back_kernel, tile, long_rows, micros),
        grid_spec=pltpu.PrefetchScalarGridSpec(
            num_scalar_prefetch=3,
            grid=(pairs,),
            in_specs=[heads_spec(0), heads_spec(1), heads_spec(2), heads_spec(0), sums_spec],
            out_specs=[heads_spec(0)] * 3,
            scratch_shapes=[pltpu.VMEM((pair, long_rows), F32)] * 2,
        ),
        out_shape=[jax.ShapeDtypeStruct((width, total), BF)] * 3,
        compiler_params=params(),
        name="attend_back",
    )(tile_len, lengths, count, triple_t, triple_t, triple_t, pulled_t, sums)

    long_grad, short_grad, entry_vector, heads_g, position_g = pl.pallas_call(
        partial(entry_kernel, tile, long_blocks),
        grid_spec=pltpu.PrefetchScalarGridSpec(
            num_scalar_prefetch=3,
            grid=(blocks,),
            in_specs=[by_column(width)] * 3
            + [by_block(width), by_block(width), whole((width, 3 * width)), whole((1, width)), whole((1, width))],
            out_specs=[long_spec, short_spec, whole((8, width)), anywhere, anywhere],
            scratch_shapes=[
                pltpu.VMEM((width, 3 * width), F32),
                pltpu.VMEM((patches, width), F32),
                pltpu.VMEM((BLOCK, width), F32),
                pltpu.VMEM((2, width, width), BF),
                pltpu.SemaphoreType.DMA((2,)),
            ],
        ),
        out_shape=[
            jax.ShapeDtypeStruct((micros * long_rows, width), BF),
            jax.ShapeDtypeStruct((short_total, width), BF),
            jax.ShapeDtypeStruct((8, width), F32),
            jax.ShapeDtypeStruct((width, 3 * width), BF),
            jax.ShapeDtypeStruct((patches, width), BF),
        ],
        compiler_params=params(),
        name="entry",
    )(
        tile_len, held, index, *grads, start, grad_middle, w["heads_weight"], lane("mixer_gain"), lane("mixer_shift"),
    )
    matrices = {
        "position": position_g, "heads_weight": heads_g, "out_weight": out_g, "up_weight": up_g,
        "down_weight": down_g, "align_weight": align_g,
    }
    vectors = {
        "up_bias": vector[0], "out_bias": vector[1, :width], "dense_gain": vector[2, :width],
        "dense_shift": vector[3, :width], "down_bias": vector[4, :width], "align_bias": vector[5, :teach],
        "query_bias": entry_vector[0], "mixer_gain": entry_vector[1], "value_bias": entry_vector[2],
        "mixer_shift": entry_vector[3],
    }
    return long_out, short_out, long_grad, short_grad, matrices, vectors


def shards(
    long_clips,
    short_clips,
    long_index,
    short_index,
    long_length,
    short_length,
    destination,
    long_target,
    short_target,
    position,
    mixer_gain,
    mixer_shift,
    heads_weight,
    query_bias,
    value_bias,
    out_weight,
    out_bias,
    dense_gain,
    dense_shift,
    up_weight,
    up_bias,
    down_weight,
    down_bias,
    align_weight,
    align_bias,
):
    peers = lax.axis_size("dp")
    copies = lax.axis_size("rep")
    mine = lax.axis_index("dp")
    own_copy = lax.axis_index("rep")
    micros, _, long_rows, width = long_clips.shape
    home_slots, tile = short_clips.shape[1:3]
    bal_slots = home_slots // 2
    slots = micros * home_slots
    weights = dict(
        zip(
            WEIGHT_NAMES,
            (
                position, mixer_gain, mixer_shift, heads_weight, query_bias, value_bias, out_weight, out_bias,
                dense_gain, dense_shift, up_weight, up_bias, down_weight, down_bias, align_weight, align_bias,
            ),
        )
    )
    group_dest = lax.dynamic_index_in_dim(
        destination.reshape(micros, peers, copies, home_slots), own_copy, 2, keepdims=False
    )
    group_len = lax.dynamic_index_in_dim(
        short_length.reshape(micros, peers, copies, home_slots), own_copy, 2, keepdims=False
    )
    own_dest = lax.dynamic_index_in_dim(group_dest, mine, 1, keepdims=False).reshape(slots)
    own_len = lax.dynamic_index_in_dim(group_len, mine, 1, keepdims=False).reshape(slots)
    lengths = long_length[:, 0]
    tile_len, source, held, count, chosen = plan_rows(lengths, own_len, tile, long_rows)
    packed_index = jnp.sum(
        jnp.where(chosen[:, :, None], short_index.reshape(1, slots, tile), 0), axis=1
    )
    index = jnp.concatenate([long_index.reshape(-1), packed_index.reshape(-1)])
    rows = jnp.concatenate([long_clips.reshape(-1, width), short_clips.reshape(-1, width)], axis=0)
    teach = long_target.shape[-1]
    targets = jnp.concatenate([long_target.reshape(-1, teach), short_target.reshape(-1, teach)], axis=0)
    long_out, short_out, long_grad, short_grad, matrices, vectors = run_block(
        rows, index, targets, tile_len, source, held, count, lengths, tile, long_rows, micros, weights
    )
    pick = chosen.astype(jnp.bfloat16)
    slot_micro = jnp.arange(slots) // home_slots
    wanted = (
        (own_dest[None, None, :] == jnp.arange(peers)[:, None, None])
        & (own_len[None, None, :] > 0)
        & (slot_micro[None, None, :] == jnp.arange(micros)[None, :, None])
    )
    send_map = jnp.einsum("pms,ks->pmk", wanted.astype(jnp.bfloat16), pick).reshape(peers * micros, slots)
    send = jnp.dot(send_map.astype(jnp.bfloat16), short_out.reshape(slots, tile * width))
    got = lax.all_to_all(
        send.reshape(peers, micros, tile, width), "dp", split_axis=0, concat_axis=0, tiled=True
    )
    slot_pick = jnp.arange(home_slots)[:, None] % bal_slots == jnp.arange(bal_slots)[None, :]
    incoming = (group_dest == mine) & (group_len > 0)
    recv_map = jnp.any(incoming[..., None] & slot_pick[None, None], axis=2)
    short_bal = jnp.einsum("mpb,pmtd->mbtd", recv_map.astype(jnp.bfloat16), got)
    short_home = jnp.dot(pick.T, short_grad.reshape(slots, tile * width))
    return (
        long_out.reshape(micros, 1, long_rows, width),
        short_bal,
        long_grad.reshape(micros, 1, long_rows, width),
        short_home.reshape(micros, home_slots, tile, width),
    ) + combine(matrices, vectors, copies)


def combine(matrices, vectors, copies):
    peers = lax.axis_size("dp")
    mine = lax.axis_index("dp")
    names = [name for name in WEIGHT_NAMES if name in vectors]
    flat = jnp.concatenate([vectors[name].reshape(peers, -1) for name in names], axis=1)
    flat = lax.psum(flat, ("dp", "rep"))
    flat = lax.dynamic_index_in_dim(flat, mine, 0, keepdims=False)
    shared = {}
    begin = 0
    for name in names:
        size = vectors[name].shape[0] // peers
        shared[name] = flat[begin : begin + size]
        begin += size
    for name, wide in matrices.items():
        rows = wide.shape[0] // peers
        padded = -(-rows // (8 * copies)) * 8 * copies
        if padded != rows:
            wide = wide.reshape(peers, rows, -1)
            wide = jnp.pad(wide, ((0, 0), (0, padded - rows), (0, 0)))
            wide = wide.reshape(peers * padded, -1)
        piece = lax.psum_scatter(wide, ("dp", "rep"), scatter_dimension=0, tiled=True)
        piece = lax.all_gather(piece, "rep", axis=0, tiled=True)[:rows]
        shared[name] = piece.astype(jnp.float32)
    return tuple(shared[name] for name in WEIGHT_NAMES)


def solution(mesh):
    placed = (
        P(None, ("dp", "rep"), None, None),
        P(None, ("dp", "rep"), None, None),
        P(None, ("dp", "rep"), None),
        P(None, ("dp", "rep"), None),
        P(None, ("dp", "rep")),
        P(),
        P(),
        P(None, ("dp", "rep"), None, None),
        P(None, ("dp", "rep"), None, None),
        P(),
        P(),
        P(),
        P(),
        P(),
        P(),
        P(),
        P(),
        P(),
        P(),
        P(),
        P(),
        P(),
        P(),
        P(),
        P(),
    )
    return jax.shard_map(
        shards,
        mesh=mesh,
        in_specs=placed,
        out_specs=(
            P(None, ("dp", "rep"), None, None),
            P(None, ("dp", "rep"), None, None),
            P(None, ("dp", "rep"), None, None),
            P(None, ("dp", "rep"), None, None),
            P("dp", None),
            P("dp"),
            P("dp"),
            P("dp", None),
            P("dp"),
            P("dp"),
            P("dp", None),
            P("dp"),
            P("dp"),
            P("dp"),
            P("dp", None),
            P("dp"),
            P("dp", None),
            P("dp"),
            P("dp", None),
            P("dp"),
        ),
        check_vma=False,
    )
```

time: 1410 us -> 957 us (0.68)
  matrix products: 675 us -> 5.84 us
  waiting for transfers between devices: 133 us -> 467 us
  Pallas kernels: 0 us -> 271 us
  other arithmetic: 278 us -> 22.8 us
  local copies, waits for them, and re-layouts: 157 us -> 32.6 us
    dot_general x70 -> x3, matrix products: 675 us -> 5.84 us  [the longest x1 2.33 us: shards(): jnp.dot(send_map.astype(jnp.bfloat16), short_out.reshape(slots, tile * wi...]
    reduce_scatter x6, waiting for transfers between devices: 133 us -> 465 us  [combine(): lax.psum_scatter(wide, ('dp', 'rep'), scatter_dimension=0, tiled=True)]
    pallas_call x0 -> x5, Pallas kernels: none -> 271 us  [the longest x1 92.1 us: run_block(): pl.pallas_call(partial(middle_kernel, tile, long_blocks), grid_spec=pltpu...]
    psum x1, blocking collectives: 3.17 us -> 125 us  [combine(): flat = lax.psum(flat, ('dp', 'rep'))]
    unnamed x1 -> x0, blocking collectives: 111 us -> none
    convert_element_type x11 -> x6, other arithmetic: 103 us -> 4.97 us  [combine(): shared[name] = piece.astype(jnp.float32)]
    reduce_sum x17 -> x5, other arithmetic: 86.9 us -> 1.8 us  [the longest x1 0.77 us: shards(): jnp.sum(jnp.where(chosen[:, :, None], short_index.reshape(1, slots, tile)...]
    slice x35 -> x7, local copies, waits for them, and re-layouts: 58.3 us -> 4.51 us  [the longest x3 1.84 us: combine(): shared[name] = flat[begin:begin + size]]
  transfers between devices with their start and end apart: 7 -> 7, of which waited for: 1 -> 5; matrix products, arithmetic and copies ran while one was open for 42% -> 3% of each run, Pallas kernels for 0% -> 11%
where the time goes in v1:
time: 957 us; the launch traced here: 958 us
  waiting for transfers between devices  467 us (49%)
  Pallas kernels  271 us (28%)
  blocking collectives  139 us (15%)
  local copies, waits for them, and re-layouts  32.6 us (3%)
  other arithmetic  22.8 us (2%)
  between operations  16.1 us (2%)
    reduce_scatter x6, waiting for transfers between devices, combine(): lax.psum_scatter(wide, ('dp', 'rep'), scatter_dimension=0, tiled=True)  465 us
    psum x1, blocking collectives, combine(): flat = lax.psum(flat, ('dp', 'rep'))  125 us
    pallas_call x1, Pallas kernels, run_block(): pl.pallas_call(partial(middle_kernel, tile, long_blocks), grid_spec=pltpu...  92.1 us
    pallas_call x1, Pallas kernels, run_block(): pl.pallas_call(partial(attend_back_kernel, tile, long_rows, micros), grid...  59.1 us
    pallas_call x1, Pallas kernels, run_block(): pl.pallas_call(partial(entry_kernel, tile, long_blocks), grid_spec=pltpu....  44.1 us
    pallas_call x1, Pallas kernels, run_block(): pl.pallas_call(partial(attend_kernel, tile, long_rows, micros), grid_spec...  44.1 us
    pallas_call x1, Pallas kernels, run_block(): pl.pallas_call(partial(project_kernel, tile), grid_spec=pltpu.PrefetchSca...  31.3 us
  transfers between devices with their start and end apart: 7, of which 5 were waited for; matrix products, arithmetic and copies ran while one was open for 3% of the time, Pallas kernels for 11%

profile of v1, /device:TPU:0, one launch (start us, length us, event | category | flops | bytes accessed | tf_op | source)
XLA Modules:
  0.0 958.1 jit_solution(14687194485462067683)
XLA Ops:
  7.3 0.8 reshape.359
  8.1 0.6 convert_reduce_fusion
  9.0 0.7 fusion.26
  9.7 0.1 select_reduce_fusion.2
  9.9 0.7 fusion.24
  10.5 0.7 subtract_clamp_fusion
  11.6 0.6 select_reduce_fusion.1.held
  13.6 0.8 select_reduce_fusion
  14.4 0.7 pad_maximum_fusion.2
  15.1 0.6 reshape.366.refs_6_
  15.8 1.3 reshape.367.refs_7_.refs_6_
  17.0 1.3 reshape.368.refs_8_.refs_7_
  18.3 1.3 reshape.371.refs_5_
  19.6 1.3 reshape.372.refs_6_
  20.8 1.3 reshape.373.refs_7_
  22.1 1.3 reshape.375.refs_11_
  23.4 0.6 pad_add_fusion.2.source
  24.0 0.6 pad_add_fusion.3.count
  24.6 1.3 pad_add_fusion.index
  25.9 4.3 pad_maximum_fusion.1.refs_0_.refs_1_.refs_2_.refs_3_
  30.1 31.3 %project.1 = (bf16[2304,2560]{1,0:T(8,128)(2,1)}, f32[2560,768]{1,0:T(8,128)}) custom-call(s32[40]{0:T(128)} %copy-done.1, s32[10]{0:T(128)} %select_reduce_fusion.1.held, s32[40]{0:T(128)} %pad_add_fusion.2.source, s32[2560]{0:T(1024)} %pad_add_fusion.index, bf16[2560,768]{1,0:T(8,128)(2,1)} %pad_maximum_fusion.1.refs_0_.refs_1_.refs_2_.refs_3_, ...), custom_call_target="tpu_custom_call" | custom-call | tf_op jit(solution)/shard_map/project/pallas_call | solution.py:569
  61.4 44.1 %attend.1 = (bf16[768,2560]{1,0:T(8,128)(2,1)}, f32[6,2,2560]{2,1,0:T(2,128)}) custom-call(s32[40]{0:T(128)} %copy-done.1, s32[2]{0:T(128)} %bitcast.86, s32[3]{0:T(128)} %pad_add_fusion.3.count, bf16[2304,2560]{1,0:T(8,128)(2,1)} %get-tuple-element.41.query.keys.values, bf16[2304,2560]{1,0:T(8,128)(2,1)} %get-tuple-element.41.query.keys.values, ...), custom_call_target="tpu_custom_call" | custom-call | tf_op jit(solution)/shard_map/attend/pallas_call | solution.py:599
  105.5 5.5 pad_maximum_fusion.refs_0_.refs_1_.refs_2_.refs_3_
  111.0 92.1 %middle.1 = (bf16[2048,768]{1,0:T(8,128)(2,1)}, bf16[512,768]{1,0:T(8,128)(2,1)}, bf16[768,2560]{1,0:T(8,128)(2,1)}, f32[2560,768]{1,0:T(8,128)}, f32[8,3072]{1,...) custom-call(s32[40]{0:T(128)} %copy-done.1, ...), custom_call_target="tpu_custom_call" | custom-call | tf_op jit(solution)/shard_map/middle/pallas_call | solution.py:615
  203.2 0.7 reduce-scatter.17.cloned.1.call-update
  203.9 59.1 %attend_back.1 = (bf16[768,2560]{1,0:T(8,128)(2,1)}, bf16[768,2560]{1,0:T(8,128)(2,1)}, bf16[768,2560]{1,0:T(8,128)(2,1)}) custom-call(s32[40]{0:T(128)} %copy-done.1, s32[2]{0:T(128)} %bitcast.87, s32[3]{0:T(128)} %pad_add_fusion.3.count, bf16[2304,2560]{1,0:T(8,128)(2,1)} %get-tuple-element.41.query.keys.values, ...), custom_call_target="tpu_custom_call" | custom-call | tf_op jit(solution)/shard_map/attend_back/pallas_call | solution.py:663
  263.0 44.1 %entry.1 = (bf16[2048,768]{1,0:T(8,128)(2,1)}, bf16[512,768]{1,0:T(8,128)(2,1)}, f32[8,768]{1,0:T(8,128)}, bf16[768,2304]{1,0:T(8,128)(2,1)}, bf16[6272,768]{1,0:T(8,128)(2,1)}) custom-call(s32[40]{0:T(128)} %copy-done.1, s32[10]{0:T(128)} %select_reduce_fusion.1.held, s32[2560]{0:T(1024)} %pad_add_fusion.index, ...), custom_call_target="tpu_custom_call" | custom-call | tf_op jit(solution)/shard_map/entry/pallas_call | solution.py:677
  307.2 0.5 reduce-scatter.13.cloned.1.call-update
  307.8 0.5 reduce-scatter.15.cloned.1.call-update
  308.4 8.2 pad.4
  316.6 1.1 copy-done
  317.7 1.2 reshape.379
  319.2 2.3 fusion.2
  321.6 2.6 copy.83
  324.2 4.0 all-to-all-start
  328.5 2.4 reshape.381
  331.0 1.6 fusion.10
  332.6 1.0 copy.88
  333.9 0.9 slice_reduce_fusion.2
  335.0 0.9 slice_reduce_fusion
  336.1 0.8 slice_reduce_fusion.1
  337.1 125.4 %psum.7 = f32[16,640]{1,0:T(8,128)S(1)} all-reduce(f32[16,640]{1,0:T(8,128)S(1)} %concatenate.31), channel_id=1, replica_groups=mesh['dp'=16,'rep'=2] {'dp','rep'}, use_global_device_ids=true, to_apply=%region_10.11 | all-reduce | flops 10240 | bytes 81920 | tf_op jit(solution)/shard_map/psum | solution.py:812
  462.5 0.6 dynamic-slice.11
  463.1 0.6 dynamic-slice_bitcast_fusion
  463.7 0.6 dynamic-slice_bitcast_fusion.1
  464.4 2.2 all_gather.20
  466.6 0.7 convert_element_type.30
  467.3 6.4 reduce-scatter.17.cloned.1.call-done
  473.6 2.1 all_gather.23
  475.7 0.7 convert_element_type.33
  476.4 104.8 %reduce-scatter.9.cloned.1.call-done = bf16[24,2304]{1,0:T(8,128)(2,1)} async-done(((bf16[768,2304]{1,0:T(8,128)(2,1)}), bf16[24,2304]{1,0:T(8,128)(2,1)}) %reduce-scatter.9.cloned.1.call-update) | async-done | bytes 110608 | tf_op jit(solution)/shard_map/reduce_scatter | solution.py:827
  581.3 2.2 all_gather.19
  583.4 0.8 convert_element_type.29
  584.2 1.9 fusion
  586.1 0.8 copy.86
  586.9 105.5 %reduce-scatter.13.cloned.1.call-done = bf16[24,3072]{1,0:T(8,128)(2,1)} async-done(((bf16[768,3072]{1,0:T(8,128)(2,1)}), bf16[24,3072]{1,0:T(8,128)(2,1)}) %reduce-scatter.13.cloned.1.call-update) | async-done | bytes 147472 | tf_op jit(solution)/shard_map/reduce_scatter | solution.py:827
  692.4 2.2 all_gather.21
  694.7 0.9 convert_element_type.31
  695.5 109.3 %reduce-scatter.15.cloned.1.call-done = bf16[96,768]{1,0:T(8,128)(2,1)} async-done(((bf16[3072,768]{1,0:T(8,128)(2,1)}), bf16[96,768]{1,0:T(8,128)(2,1)}) %reduce-scatter.15.cloned.1.call-update) | async-done | bytes 147472 | tf_op jit(solution)/shard_map/reduce_scatter | solution.py:827
  804.8 2.2 all_gather.22
  807.0 0.9 convert_element_type.32
  807.8 139.4 %reduce-scatter.7.cloned.1.call-done = bf16[200,768]{1,0:T(8,128)(2,1)} async-done(((bf16[6400,768]{1,0:T(8,128)(2,1)}), bf16[200,768]{1,0:T(8,128)(2,1)}) %reduce-scatter.7.cloned.1.call-update) | async-done | bytes 307216 | tf_op jit(solution)/shard_map/reduce_scatter | solution.py:827
  947.2 2.4 all_gather.18
  949.7 1.1 slice_convert_fusion
  (60 shorter events, 2.7 us)
Async XLA Ops:
  7.2 457.2 %reduce-scatter.11.cloned.1.call-start = ((), (), s32[]{:S(2)}) async-start(), calls=%async_computation.9 | async-start | bytes 1216512 | tf_op jit(solution)/shard_map/reduce_scatter | solution.py:827
  11.4 18.7 %copy-start.1 = (s32[40]{0:T(128)}, s32[40]{0:T(128)S(1)}, u32[]{:S(2)}) copy-start(s32[40]{0:T(128)S(1)} %pad_add_fusion.1.tile_len) | copy-start | bytes 484
  203.1 270.5 %reduce-scatter.17.cloned.1.call-start = ((), (), s32[]{:S(2)}) async-start(), calls=%async_computation.12 | async-start | bytes 1622016 | tf_op jit(solution)/shard_map/reduce_scatter | solution.py:827
  203.9 377.4 %reduce-scatter.9.cloned.1.call-start = ((), (), s32[]{:S(2)}) async-start(), calls=%async_computation.8 | async-start | bytes 3649536 | tf_op jit(solution)/shard_map/reduce_scatter | solution.py:827
  307.2 385.3 %reduce-scatter.13.cloned.1.call-start = ((), (), s32[]{:S(2)}) async-start(), calls=%async_computation.10 | async-start | bytes 4866048 | tf_op jit(solution)/shard_map/reduce_scatter | solution.py:827
  307.8 497.0 %reduce-scatter.15.cloned.1.call-start = ((), (), s32[]{:S(2)}) async-start(), calls=%async_computation.11 | async-start | bytes 4866048 | tf_op jit(solution)/shard_map/reduce_scatter | solution.py:827
  308.3 638.9 %reduce-scatter.7.cloned.1.call-start = ((), (), s32[]{:S(2)}) async-start(), calls=%async_computation.7 | async-start | bytes 10137600 | tf_op jit(solution)/shard_map/reduce_scatter | solution.py:827
  316.5 1.1 copy-start
  316.5 2.4 copy-start.3
  324.2 260.0 %all-to-all-start = ((bf16[16,2,64,768]{3,2,1,0:T(8,128)(2,1)}), bf16[16,2,64,768]{3,2,1,0:T(8,128)(2,1)S(1)}, u32[]{:S(2)}, u32[]{:S(2)}) async-start(bf16[16,2,64,768]{3,2,1,0:T(8,128)(2,1)} %copy.83), calls=%async_computation | async-start | bytes 6291456 | tf_op jit(solution)/shard_map/all_to_all | solution.py:791
  328.2 5.3 copy-start.2
Sparse Core Ops, SparseCore 0:
  203.3 155.2 reduce-scatter.10
  363.8 109.8 reduce-scatter.16
  479.1 102.1 reduce-scatter.8
  586.6 105.8 reduce-scatter.12
  698.7 106.0 reduce-scatter.14
  810.6 136.6 reduce-scatter.6
